TPU v7x, 32 devices: a whole 2x2x4 slice. The times are simulated.
32 devices in a mesh: grp: 2 (over y), tile: 4 (over z), sub: 4 (over x, core).
Axes of the slice: x: 2, y: 2, z: 4, core: 2. Of those that a mesh axis runs over, the one named last changes fastest.
Arguments:
- features: bfloat16 [24, 32, 1024], P(('grp', 'tile'), 'sub'), parts along dimension 0, may hold values from -6 to 6
- out_grad: bfloat16 [24, 32, 1024], P(('grp', 'tile'), 'sub'), parts along dimension 0, may hold values from -6 to 6
- filters: bfloat16 [5, 32, 32], replicated, may hold values from -0.5 to 0.5
- tile_map: int32 [12], replicated, may hold values from 0 to 11, as said below
Outputs:
- in_grad: bfloat16 [24, 32, 1024], P(('grp', 'tile'), 'sub'), parts along dimension 0
- weight_grad: float32 [10, 32, 32], P('grp', 'sub'), parts along dimension 0
There are 2 independent parts, one for each index of `grp`. A program takes and returns all parts, laid end to end along the dimension named above; an argument that names none is the same for every part. Nothing has to cross between parts.
Inputs may be any that keep to these rules, and one draw needn't show every extreme that they name: tile_map[s] is the nested index of the tile held in slot s; slots 3 * j to 3 * j + 2 lie on index j of tile and hold the nested indices 3 * j to 3 * j + 2 in some order.
All inputs are finite; a program needn't handle non-finite values.
Results may differ from a plain program's by a relative error of at most 0.00045.
Values may be sent and summed in bfloat16 or wider, within the bound.
No kernel may reach another device: no remote copies, remote signals or barrier semaphores. Data moves between devices by JAX's collectives and lax.ppermute only.
A program may use at most 64 MiB of HBM per device.

v0:
```python
import math
import jax
import jax.numpy as jnp
import numpy as np
from jax import lax
from jax.sharding import PartitionSpec as P

K = 5


def from_behind(value, axis, steps):
    count = lax.axis_size(axis)
    pairs = [(source, (source + steps) % count) for source in range(count)]
    return lax.ppermute(value, axis, pairs)


def tile_coords(nested_code, bit_count):
    coord_x = nested_code * 0
    coord_y = nested_code * 0
    for bit_level in range(bit_count):
        coord_x = coord_x + nested_code // 4**bit_level % 2 * 2**bit_level
        coord_y = coord_y + nested_code // (2 * 4**bit_level) % 2 * 2**bit_level
    return (coord_x, coord_y)


def nested_index(coord_x, coord_y, bit_count):
    nested_code = coord_x * 0
    for bit_level in range(bit_count):
        nested_code = nested_code + coord_x // 2**bit_level % 2 * 4**bit_level
        nested_code = nested_code + coord_y // 2**bit_level % 2 * (2 * 4**bit_level)
    return nested_code


def pick(condition, when_true, when_false):
    return when_false + (when_true - when_false) * condition


def neighbour_codes(tile_ids, per_face, side_count):
    bit_count = side_count.bit_length() - 1
    face_id = tile_ids // per_face
    coord_x, coord_y = tile_coords(tile_ids % per_face, bit_count)
    column = face_id % 4
    is_north = face_id < 4
    is_south = face_id >= 8
    last_tile = side_count - 1

    def by_cycle(north_value, equator_value, south_value):
        return pick(is_north, north_value, pick(is_south, south_value, equator_value))

    side_rules = [
        (
            coord_x > 0,
            (face_id, coord_x - 1, coord_y, 1),
            (
                by_cycle(4 + column, 8 + (column + 3) % 4, 8 + (column + 3) % 4),
                by_cycle(last_tile, last_tile, coord_y),
                by_cycle(coord_y, coord_y, 0),
                by_cycle(1, 1, 2),
            ),
        ),
        (
            coord_x < last_tile,
            (face_id, coord_x + 1, coord_y, 0),
            (
                by_cycle((column + 1) % 4, column, 4 + (column + 1) % 4),
                by_cycle(coord_y, 0, 0),
                by_cycle(last_tile, coord_y, coord_y),
                by_cycle(3, 0, 0),
            ),
        ),
        (
            coord_y > 0,
            (face_id, coord_x, coord_y - 1, 3),
            (
                by_cycle(4 + (column + 1) % 4, 8 + column, 8 + (column + 1) % 4),
                by_cycle(coord_x, coord_x, 0),
                by_cycle(last_tile, last_tile, coord_x),
                by_cycle(3, 3, 0),
            ),
        ),
        (
            coord_y < last_tile,
            (face_id, coord_x, coord_y + 1, 2),
            (
                by_cycle((column + 3) % 4, (column + 3) % 4, 4 + column),
                by_cycle(last_tile, coord_x, coord_x),
                by_cycle(coord_x, 0, 0),
                by_cycle(1, 2, 2),
            ),
        ),
    ]
    target_list = []
    edge_list = []
    for inside, within, across in side_rules:
        chosen = [
            pick(inside, near_value, far_value) for near_value, far_value in zip(within, across)
        ]
        target_list.append(chosen[0] * per_face + nested_index(chosen[1], chosen[2], bit_count))
        edge_list.append(chosen[3] + tile_ids * 0)
    return (target_list, edge_list)


def neighbour_table(tile_map, per_face, side_count):
    target_list, edge_list = neighbour_codes(tile_map, per_face, side_count)
    targets = jnp.stack(target_list, axis=1).astype(jnp.int32)
    edges = jnp.stack(edge_list, axis=1).astype(jnp.int32)
    slot_of = jnp.argsort(tile_map).astype(jnp.int32)
    return (slot_of[targets].astype(jnp.int32), edges)


def peer_offsets(slot_count, device_count, per_face, side_count):
    tile_ids = np.arange(slot_count * device_count, dtype=np.int64)
    target_list, edge_list = neighbour_codes(tile_ids, per_face, side_count)
    targets = np.stack(target_list, axis=1)
    offsets = (tile_ids[:, None] // slot_count - targets // slot_count) % device_count
    distinct = sorted(set((int(value) for value in offsets.ravel())) - {0})
    position = np.zeros(device_count, dtype=np.int32)
    for order, value in enumerate(distinct):
        position[value] = order + 1
    return (distinct, position)


def edge_lines(values, tile_side):
    return jnp.stack(
        [
            values[..., :tile_side],
            values[..., -tile_side:],
            values[..., ::tile_side],
            values[..., tile_side - 1 :: tile_side],
        ],
        axis=1,
    )


def stencil(values, ghosts, tile_side):
    position = jnp.arange(values.shape[-1]) % tile_side
    zero_line = jnp.zeros_like(values[..., :1])
    upper_side = jnp.concatenate([ghosts[:, 0], values[..., :-tile_side]], axis=-1)
    lower_side = jnp.concatenate([values[..., tile_side:], ghosts[:, 1]], axis=-1)
    left_side = jnp.where(
        position == 0,
        jnp.repeat(ghosts[:, 2], tile_side, axis=-1),
        jnp.concatenate([zero_line, values[..., :-1]], axis=-1),
    )
    right_side = jnp.where(
        position == tile_side - 1,
        jnp.repeat(ghosts[:, 3], tile_side, axis=-1),
        jnp.concatenate([values[..., 1:], zero_line], axis=-1),
    )
    return -0.25 * (upper_side + lower_side + left_side + right_side)


def tile_total(filter_part):
    return lax.psum(filter_part, "tile")


def on_device(features, out_grad, filters, tile_map):
    slot_count = features.shape[0]
    group_channels = features.shape[1]
    tile_side = math.isqrt(features.shape[2])
    device_count = lax.axis_size("tile")
    total_tiles = slot_count * device_count
    side_count = math.isqrt(total_tiles // 12)
    scale_factor = 1.0 / math.sqrt(total_tiles * features.shape[2])
    highest = lax.Precision.HIGHEST
    slot_table, edge_table = neighbour_table(tile_map, total_tiles // 12, side_count)
    my_device = lax.axis_index("tile")
    first_slot = my_device * slot_count
    my_slots = lax.dynamic_slice_in_dim(slot_table, first_slot, slot_count, 0)
    my_edges = lax.dynamic_slice_in_dim(edge_table, first_slot, slot_count, 0)
    channel_start = lax.axis_index("sub") * group_channels
    weights = filters.astype(jnp.float32)
    distinct, position = peer_offsets(slot_count, device_count, total_tiles // 12, side_count)
    sender_gap = (my_device - my_slots // slot_count) % device_count
    local_rows = jnp.asarray(position)[sender_gap] * slot_count + my_slots % slot_count

    def laplace(values):
        border = edge_lines(values, tile_side).reshape(slot_count, 4, group_channels * tile_side)
        received = [border]
        for offset_value in distinct:
            received.append(from_behind(border, "tile", offset_value))
        stacked = jnp.concatenate(received, axis=0)
        stacked = stacked.reshape(stacked.shape[0], 4, group_channels, tile_side)
        ghosts = stacked[local_rows, my_edges]
        return stencil(values, ghosts, tile_side)

    whole_grad = lax.all_gather(out_grad, "sub", axis=1, tiled=True)
    cotangent = whole_grad.astype(jnp.float32)
    inputs = features.astype(jnp.float32)
    previous, current = (inputs, laplace(inputs))
    filter_terms = [
        jnp.einsum("sip,sop->io", inputs, cotangent, precision=highest),
        jnp.einsum("sip,sop->io", current, cotangent, precision=highest),
    ]
    for degree in range(2, K):
        previous, current = (current, 2.0 * laplace(current) - previous)
        filter_terms.append(jnp.einsum("sip,sop->io", current, cotangent, precision=highest))
    weight_grad = tile_total(jnp.stack(filter_terms)) * scale_factor
    row_block = lax.dynamic_slice_in_dim(weights, channel_start, group_channels, 1)

    def mixed(degree):
        return jnp.einsum("sop,io->sip", cotangent, row_block[degree], precision=highest)

    next_sum = mixed(K - 1)
    after_next = jnp.zeros_like(next_sum)
    for degree in range(K - 2, 0, -1):
        next_sum, after_next = (mixed(degree) + 2.0 * laplace(next_sum) - after_next, next_sum)
    in_grad = (mixed(0) + laplace(next_sum) - after_next).astype(jnp.bfloat16)
    return (in_grad, weight_grad)


def solution(mesh):
    placed = (P(("grp", "tile"), "sub", None), P(("grp", "tile"), "sub", None), P(), P())
    return jax.shard_map(
        on_device,
        mesh=mesh,
        in_specs=placed,
        out_specs=(P(("grp", "tile"), "sub", None), P("grp", "sub", None)),
        check_vma=False,
    )
```

profile of v0, /device:TPU:0, one launch (start us, length us, event | category | flops | bytes accessed | tf_op | source)
XLA Modules:
  0.0 89.9 jit_solution(3915343842741492382)
XLA Ops:
  0.7 0.8 fusion.100
  2.1 3.1 %collective-permute-start.12 = (f32[3,4,256]{2,0,1:T(4,128)S(1)}, f32[3,4,256]{2,0,1:T(4,128)S(1)}, u32[]{:S(2)}, u32[]{:S(2)}) collective-permute-start(f32[3,4,256]{2,0,1:T(4,128)S(1)} %constant_dynamic-update-slice_fusion.16), channel_id=1, source_target_pairs={{0,4},{4,8},{8,12},{12,0},{1,5},{5,9},{9,13},{13,1},{2,6},{6,10},{... | collective-permute-start | bytes 36872 | tf_op jit(solution)/shard_map/ppermute | solution.py:14
  5.2 2.6 %collective-permute-start.13 = (f32[3,4,256]{2,0,1:T(4,128)S(1)}, f32[3,4,256]{2,0,1:T(4,128)S(1)}, u32[]{:S(2)}, u32[]{:S(2)}) collective-permute-start(f32[3,4,256]{2,0,1:T(4,128)S(1)} %constant_dynamic-update-slice_fusion.16), channel_id=1, source_target_pairs={{0,8},{4,12},{8,0},{12,4},{1,9},{5,13},{9,1},{13,5},{2,10},{6,14},... | collective-permute-start | bytes 36872 | tf_op jit(solution)/shard_map/ppermute | solution.py:14
  7.8 1.3 %collective-permute-start.14 = (f32[3,4,256]{2,0,1:T(4,128)S(1)}, f32[3,4,256]{2,0,1:T(4,128)S(1)}, u32[]{:S(2)}, u32[]{:S(2)}) collective-permute-start(f32[3,4,256]{2,0,1:T(4,128)S(1)} %constant_dynamic-update-slice_fusion.16), channel_id=1, source_target_pairs={{0,12},{4,0},{8,4},{12,8},{1,13},{5,1},{9,5},{13,9},{2,14},{6,2},{... | collective-permute-start | bytes 36872 | tf_op jit(solution)/shard_map/ppermute | solution.py:14
  9.2 5.6 %all_gather.3 = bf16[3,32,1024]{2,1,0:T(8,128)(2,1)S(1)} all-gather(bf16[3,8,1024]{2,1,0:T(8,128)(2,1)S(1)} %copy-done.2), channel_id=1, replica_groups=mesh['grp'=2,'tile'=4,'sub'=4] {'sub'}, dimensions={1}, use_global_device_ids=true | all-gather | bytes 245760 | tf_op jit(solution)/shard_map/all_gather | solution.py:187
  15.7 0.7 collective-permute-start
  18.3 1.2 %sort.17 = (s32[12]{0:T(128)}, s32[12]{0:T(128)S(1)}) sort(s32[12]{0:T(128)S(1)} %copy-done.3, s32[12]{0:T(128)S(1)} %iota.45), dimensions={0}, to_apply=%region_0.1 | sort | flops 48 | bytes 192 | tf_op jit(solution)/shard_map/jit(argsort)/sort | solution.py:107
  19.6 0.8 gather_fusion
  21.4 2.8 %collective-permute-start.2 = (f32[3,4,256]{2,0,1:T(4,128)S(1)}, f32[3,4,256]{2,0,1:T(4,128)S(1)}, u32[]{:S(2)}, u32[]{:S(2)}) collective-permute-start(f32[3,4,256]{2,0,1:T(4,128)S(1)} %constant_dynamic-update-slice_fusion), channel_id=1, source_target_pairs={{0,12},{4,0},{8,4},{12,8},{1,13},{5,1},{9,5},{13,9},{2,14},{6,2},{... | collective-permute-start | bytes 36872 | tf_op jit(solution)/shard_map/ppermute | solution.py:14
  27.3 1.5 %collective-permute-start.16 = (f32[3,4,256]{2,0,1:T(4,128)S(1)}, f32[3,4,256]{2,0,1:T(4,128)S(1)}, u32[]{:S(2)}, u32[]{:S(2)}) collective-permute-start(f32[3,4,256]{2,0,1:T(4,128)S(1)} %constant_dynamic-update-slice_fusion.20), channel_id=1, source_target_pairs={{0,8},{4,12},{8,0},{12,4},{1,9},{5,13},{9,1},{13,5},{2,10},{6,14},... | collective-permute-start | bytes 36872 | tf_op jit(solution)/shard_map/ppermute | solution.py:14
  29.0 2.9 %collective-permute-start.17 = (f32[3,4,256]{2,0,1:T(4,128)S(1)}, f32[3,4,256]{2,0,1:T(4,128)S(1)}, u32[]{:S(2)}, u32[]{:S(2)}) collective-permute-start(f32[3,4,256]{2,0,1:T(4,128)S(1)} %constant_dynamic-update-slice_fusion.20), channel_id=1, source_target_pairs={{0,12},{4,0},{8,4},{12,8},{1,13},{5,1},{9,5},{13,9},{2,14},{6,2},{... | collective-permute-start | bytes 36872 | tf_op jit(solution)/shard_map/ppermute | solution.py:14
  34.4 1.0 %collective-permute-start.4 = (f32[3,4,256]{2,0,1:T(4,128)S(1)}, f32[3,4,256]{2,0,1:T(4,128)S(1)}, u32[]{:S(2)}, u32[]{:S(2)}) collective-permute-start(f32[3,4,256]{2,0,1:T(4,128)S(1)} %constant_dynamic-update-slice_fusion.4), channel_id=1, source_target_pairs={{0,8},{4,12},{8,0},{12,4},{1,9},{5,13},{9,1},{13,5},{2,10},{6,14},... | collective-permute-start | bytes 36872 | tf_op jit(solution)/shard_map/ppermute | solution.py:14
  35.8 2.9 %collective-permute-start.5 = (f32[3,4,256]{2,0,1:T(4,128)S(1)}, f32[3,4,256]{2,0,1:T(4,128)S(1)}, u32[]{:S(2)}, u32[]{:S(2)}) collective-permute-start(f32[3,4,256]{2,0,1:T(4,128)S(1)} %constant_dynamic-update-slice_fusion.4), channel_id=1, source_target_pairs={{0,12},{4,0},{8,4},{12,8},{1,13},{5,1},{9,5},{13,9},{2,14},{6,2},{... | collective-permute-start | bytes 36872 | tf_op jit(solution)/shard_map/ppermute | solution.py:14
  41.8 1.5 %collective-permute-start.19 = (f32[3,4,256]{2,0,1:T(4,128)S(1)}, f32[3,4,256]{2,0,1:T(4,128)S(1)}, u32[]{:S(2)}, u32[]{:S(2)}) collective-permute-start(f32[3,4,256]{2,0,1:T(4,128)S(1)} %constant_dynamic-update-slice_fusion.24), channel_id=1, source_target_pairs={{0,8},{4,12},{8,0},{12,4},{1,9},{5,13},{9,1},{13,5},{2,10},{6,14},... | collective-permute-start | bytes 36872 | tf_op jit(solution)/shard_map/ppermute | solution.py:14
  43.5 2.9 %collective-permute-start.20 = (f32[3,4,256]{2,0,1:T(4,128)S(1)}, f32[3,4,256]{2,0,1:T(4,128)S(1)}, u32[]{:S(2)}, u32[]{:S(2)}) collective-permute-start(f32[3,4,256]{2,0,1:T(4,128)S(1)} %constant_dynamic-update-slice_fusion.24), channel_id=1, source_target_pairs={{0,12},{4,0},{8,4},{12,8},{1,13},{5,1},{9,5},{13,9},{2,14},{6,2},{... | collective-permute-start | bytes 36872 | tf_op jit(solution)/shard_map/ppermute | solution.py:14
  48.9 1.0 %collective-permute-start.7 = (f32[3,4,256]{2,0,1:T(4,128)S(1)}, f32[3,4,256]{2,0,1:T(4,128)S(1)}, u32[]{:S(2)}, u32[]{:S(2)}) collective-permute-start(f32[3,4,256]{2,0,1:T(4,128)S(1)} %constant_dynamic-update-slice_fusion.8), channel_id=1, source_target_pairs={{0,8},{4,12},{8,0},{12,4},{1,9},{5,13},{9,1},{13,5},{2,10},{6,14},... | collective-permute-start | bytes 36872 | tf_op jit(solution)/shard_map/ppermute | solution.py:14
  50.3 2.9 %collective-permute-start.8 = (f32[3,4,256]{2,0,1:T(4,128)S(1)}, f32[3,4,256]{2,0,1:T(4,128)S(1)}, u32[]{:S(2)}, u32[]{:S(2)}) collective-permute-start(f32[3,4,256]{2,0,1:T(4,128)S(1)} %constant_dynamic-update-slice_fusion.8), channel_id=1, source_target_pairs={{0,12},{4,0},{8,4},{12,8},{1,13},{5,1},{9,5},{13,9},{2,14},{6,2},{... | collective-permute-start | bytes 36872 | tf_op jit(solution)/shard_map/ppermute | solution.py:14
  56.3 1.5 %collective-permute-start.22 = (f32[3,4,256]{2,0,1:T(4,128)S(1)}, f32[3,4,256]{2,0,1:T(4,128)S(1)}, u32[]{:S(2)}, u32[]{:S(2)}) collective-permute-start(f32[3,4,256]{2,0,1:T(4,128)S(1)} %constant_dynamic-update-slice_fusion.28), channel_id=1, source_target_pairs={{0,8},{4,12},{8,0},{12,4},{1,9},{5,13},{9,1},{13,5},{2,10},{6,14},... | collective-permute-start | bytes 36872 | tf_op jit(solution)/shard_map/ppermute | solution.py:14
  58.0 2.9 %collective-permute-start.23 = (f32[3,4,256]{2,0,1:T(4,128)S(1)}, f32[3,4,256]{2,0,1:T(4,128)S(1)}, u32[]{:S(2)}, u32[]{:S(2)}) collective-permute-start(f32[3,4,256]{2,0,1:T(4,128)S(1)} %constant_dynamic-update-slice_fusion.28), channel_id=1, source_target_pairs={{0,12},{4,0},{8,4},{12,8},{1,13},{5,1},{9,5},{13,9},{2,14},{6,2},{... | collective-permute-start | bytes 36872 | tf_op jit(solution)/shard_map/ppermute | solution.py:14
  63.3 1.0 %collective-permute-start.10 = (f32[3,4,256]{2,0,1:T(4,128)S(1)}, f32[3,4,256]{2,0,1:T(4,128)S(1)}, u32[]{:S(2)}, u32[]{:S(2)}) collective-permute-start(f32[3,4,256]{2,0,1:T(4,128)S(1)} %constant_dynamic-update-slice_fusion.12), channel_id=1, source_target_pairs={{0,8},{4,12},{8,0},{12,4},{1,9},{5,13},{9,1},{13,5},{2,10},{6,14},... | collective-permute-start | bytes 36872 | tf_op jit(solution)/shard_map/ppermute | solution.py:14
  64.3 0.9 %collective-permute-start.11 = (f32[3,4,256]{2,0,1:T(4,128)S(1)}, f32[3,4,256]{2,0,1:T(4,128)S(1)}, u32[]{:S(2)}, u32[]{:S(2)}) collective-permute-start(f32[3,4,256]{2,0,1:T(4,128)S(1)} %constant_dynamic-update-slice_fusion.12), channel_id=1, source_target_pairs={{0,12},{4,0},{8,4},{12,8},{1,13},{5,1},{9,5},{13,9},{2,14},{6,2},{... | collective-permute-start | bytes 36872 | tf_op jit(solution)/shard_map/ppermute | solution.py:14
  65.7 1.1 %collective-permute-start.9 = (f32[3,4,256]{2,0,1:T(4,128)S(1)}, f32[3,4,256]{2,0,1:T(4,128)S(1)}, u32[]{:S(2)}, u32[]{:S(2)}) collective-permute-start(f32[3,4,256]{2,0,1:T(4,128)S(1)} %constant_dynamic-update-slice_fusion.12), channel_id=1, source_target_pairs={{0,4},{4,8},{8,12},{12,0},{1,5},{5,9},{9,13},{13,1},{2,6},{6,10},{... | collective-permute-start | bytes 36872 | tf_op jit(solution)/shard_map/ppermute | solution.py:14
  68.7 18.3 %psum.7 = f32[5,8,32]{2,1,0:T(8,128)S(1)} all-reduce(f32[5,8,32]{2,1,0:T(8,128)S(1)} %fusion.8), channel_id=1, replica_groups=mesh['grp'=2,'tile'=4,'sub'=4] {'tile'}, use_global_device_ids=true, to_apply=%region_1.2 | all-reduce | flops 1280 | bytes 10240 | tf_op jit(solution)/shard_map/psum | solution.py:154
  89.2 0.8 fusion.7
  (247 shorter events, 26.3 us)
Async XLA Ops:
  2.1 19.3 %collective-permute-start.12 = (f32[3,4,256]{2,0,1:T(4,128)S(1)}, f32[3,4,256]{2,0,1:T(4,128)S(1)}, u32[]{:S(2)}, u32[]{:S(2)}) collective-permute-start(f32[3,4,256]{2,0,1:T(4,128)S(1)} %constant_dynamic-update-slice_fusion.16), channel_id=1, source_target_pairs={{0,4},{4,8},{8,12},{12,0},{1,5},{5,9},{9,13},{13,1},{2,6},{6,10},{... | collective-permute-start | bytes 36872 | tf_op jit(solution)/shard_map/ppermute | solution.py:14
  5.2 19.0 %collective-permute-start.13 = (f32[3,4,256]{2,0,1:T(4,128)S(1)}, f32[3,4,256]{2,0,1:T(4,128)S(1)}, u32[]{:S(2)}, u32[]{:S(2)}) collective-permute-start(f32[3,4,256]{2,0,1:T(4,128)S(1)} %constant_dynamic-update-slice_fusion.16), channel_id=1, source_target_pairs={{0,8},{4,12},{8,0},{12,4},{1,9},{5,13},{9,1},{13,5},{2,10},{6,14},... | collective-permute-start | bytes 36872 | tf_op jit(solution)/shard_map/ppermute | solution.py:14
  7.8 16.4 %collective-permute-start.14 = (f32[3,4,256]{2,0,1:T(4,128)S(1)}, f32[3,4,256]{2,0,1:T(4,128)S(1)}, u32[]{:S(2)}, u32[]{:S(2)}) collective-permute-start(f32[3,4,256]{2,0,1:T(4,128)S(1)} %constant_dynamic-update-slice_fusion.16), channel_id=1, source_target_pairs={{0,12},{4,0},{8,4},{12,8},{1,13},{5,1},{9,5},{13,9},{2,14},{6,2},{... | collective-permute-start | bytes 36872 | tf_op jit(solution)/shard_map/ppermute | solution.py:14
  15.7 13.3 %collective-permute-start = (f32[3,4,256]{2,0,1:T(4,128)S(1)}, f32[3,4,256]{2,0,1:T(4,128)S(1)}, u32[]{:S(2)}, u32[]{:S(2)}) collective-permute-start(f32[3,4,256]{2,0,1:T(4,128)S(1)} %constant_dynamic-update-slice_fusion), channel_id=1, source_target_pairs={{0,4},{4,8},{8,12},{12,0},{1,5},{5,9},{9,13},{13,1},{2,6},{6,10},{... | collective-permute-start | bytes 36872 | tf_op jit(solution)/shard_map/ppermute | solution.py:14
  16.4 15.5 %collective-permute-start.1 = (f32[3,4,256]{2,0,1:T(4,128)S(1)}, f32[3,4,256]{2,0,1:T(4,128)S(1)}, u32[]{:S(2)}, u32[]{:S(2)}) collective-permute-start(f32[3,4,256]{2,0,1:T(4,128)S(1)} %constant_dynamic-update-slice_fusion), channel_id=1, source_target_pairs={{0,8},{4,12},{8,0},{12,4},{1,9},{5,13},{9,1},{13,5},{2,10},{6,14},... | collective-permute-start | bytes 36872 | tf_op jit(solution)/shard_map/ppermute | solution.py:14
  21.4 10.5 %collective-permute-start.2 = (f32[3,4,256]{2,0,1:T(4,128)S(1)}, f32[3,4,256]{2,0,1:T(4,128)S(1)}, u32[]{:S(2)}, u32[]{:S(2)}) collective-permute-start(f32[3,4,256]{2,0,1:T(4,128)S(1)} %constant_dynamic-update-slice_fusion), channel_id=1, source_target_pairs={{0,12},{4,0},{8,4},{12,8},{1,13},{5,1},{9,5},{13,9},{2,14},{6,2},{... | collective-permute-start | bytes 36872 | tf_op jit(solution)/shard_map/ppermute | solution.py:14
  26.7 9.2 %collective-permute-start.15 = (f32[3,4,256]{2,0,1:T(4,128)S(1)}, f32[3,4,256]{2,0,1:T(4,128)S(1)}, u32[]{:S(2)}, u32[]{:S(2)}) collective-permute-start(f32[3,4,256]{2,0,1:T(4,128)S(1)} %constant_dynamic-update-slice_fusion.20), channel_id=1, source_target_pairs={{0,4},{4,8},{8,12},{12,0},{1,5},{5,9},{9,13},{13,1},{2,6},{6,10},{... | collective-permute-start | bytes 36872 | tf_op jit(solution)/shard_map/ppermute | solution.py:14
  27.3 11.4 %collective-permute-start.16 = (f32[3,4,256]{2,0,1:T(4,128)S(1)}, f32[3,4,256]{2,0,1:T(4,128)S(1)}, u32[]{:S(2)}, u32[]{:S(2)}) collective-permute-start(f32[3,4,256]{2,0,1:T(4,128)S(1)} %constant_dynamic-update-slice_fusion.20), channel_id=1, source_target_pairs={{0,8},{4,12},{8,0},{12,4},{1,9},{5,13},{9,1},{13,5},{2,10},{6,14},... | collective-permute-start | bytes 36872 | tf_op jit(solution)/shard_map/ppermute | solution.py:14
  29.0 9.7 %collective-permute-start.17 = (f32[3,4,256]{2,0,1:T(4,128)S(1)}, f32[3,4,256]{2,0,1:T(4,128)S(1)}, u32[]{:S(2)}, u32[]{:S(2)}) collective-permute-start(f32[3,4,256]{2,0,1:T(4,128)S(1)} %constant_dynamic-update-slice_fusion.20), channel_id=1, source_target_pairs={{0,12},{4,0},{8,4},{12,8},{1,13},{5,1},{9,5},{13,9},{2,14},{6,2},{... | collective-permute-start | bytes 36872 | tf_op jit(solution)/shard_map/ppermute | solution.py:14
  34.3 9.1 %collective-permute-start.3 = (f32[3,4,256]{2,0,1:T(4,128)S(1)}, f32[3,4,256]{2,0,1:T(4,128)S(1)}, u32[]{:S(2)}, u32[]{:S(2)}) collective-permute-start(f32[3,4,256]{2,0,1:T(4,128)S(1)} %constant_dynamic-update-slice_fusion.4), channel_id=1, source_target_pairs={{0,4},{4,8},{8,12},{12,0},{1,5},{5,9},{9,13},{13,1},{2,6},{6,10},{... | collective-permute-start | bytes 36872 | tf_op jit(solution)/shard_map/ppermute | solution.py:14
  34.4 12.0 %collective-permute-start.4 = (f32[3,4,256]{2,0,1:T(4,128)S(1)}, f32[3,4,256]{2,0,1:T(4,128)S(1)}, u32[]{:S(2)}, u32[]{:S(2)}) collective-permute-start(f32[3,4,256]{2,0,1:T(4,128)S(1)} %constant_dynamic-update-slice_fusion.4), channel_id=1, source_target_pairs={{0,8},{4,12},{8,0},{12,4},{1,9},{5,13},{9,1},{13,5},{2,10},{6,14},... | collective-permute-start | bytes 36872 | tf_op jit(solution)/shard_map/ppermute | solution.py:14
  35.8 10.6 %collective-permute-start.5 = (f32[3,4,256]{2,0,1:T(4,128)S(1)}, f32[3,4,256]{2,0,1:T(4,128)S(1)}, u32[]{:S(2)}, u32[]{:S(2)}) collective-permute-start(f32[3,4,256]{2,0,1:T(4,128)S(1)} %constant_dynamic-update-slice_fusion.4), channel_id=1, source_target_pairs={{0,12},{4,0},{8,4},{12,8},{1,13},{5,1},{9,5},{13,9},{2,14},{6,2},{... | collective-permute-start | bytes 36872 | tf_op jit(solution)/shard_map/ppermute | solution.py:14
  41.2 9.2 %collective-permute-start.18 = (f32[3,4,256]{2,0,1:T(4,128)S(1)}, f32[3,4,256]{2,0,1:T(4,128)S(1)}, u32[]{:S(2)}, u32[]{:S(2)}) collective-permute-start(f32[3,4,256]{2,0,1:T(4,128)S(1)} %constant_dynamic-update-slice_fusion.24), channel_id=1, source_target_pairs={{0,4},{4,8},{8,12},{12,0},{1,5},{5,9},{9,13},{13,1},{2,6},{6,10},{... | collective-permute-start | bytes 36872 | tf_op jit(solution)/shard_map/ppermute | solution.py:14
  41.8 11.4 %collective-permute-start.19 = (f32[3,4,256]{2,0,1:T(4,128)S(1)}, f32[3,4,256]{2,0,1:T(4,128)S(1)}, u32[]{:S(2)}, u32[]{:S(2)}) collective-permute-start(f32[3,4,256]{2,0,1:T(4,128)S(1)} %constant_dynamic-update-slice_fusion.24), channel_id=1, source_target_pairs={{0,8},{4,12},{8,0},{12,4},{1,9},{5,13},{9,1},{13,5},{2,10},{6,14},... | collective-permute-start | bytes 36872 | tf_op jit(solution)/shard_map/ppermute | solution.py:14
  43.5 9.7 %collective-permute-start.20 = (f32[3,4,256]{2,0,1:T(4,128)S(1)}, f32[3,4,256]{2,0,1:T(4,128)S(1)}, u32[]{:S(2)}, u32[]{:S(2)}) collective-permute-start(f32[3,4,256]{2,0,1:T(4,128)S(1)} %constant_dynamic-update-slice_fusion.24), channel_id=1, source_target_pairs={{0,12},{4,0},{8,4},{12,8},{1,13},{5,1},{9,5},{13,9},{2,14},{6,2},{... | collective-permute-start | bytes 36872 | tf_op jit(solution)/shard_map/ppermute | solution.py:14
  48.8 9.1 %collective-permute-start.6 = (f32[3,4,256]{2,0,1:T(4,128)S(1)}, f32[3,4,256]{2,0,1:T(4,128)S(1)}, u32[]{:S(2)}, u32[]{:S(2)}) collective-permute-start(f32[3,4,256]{2,0,1:T(4,128)S(1)} %constant_dynamic-update-slice_fusion.8), channel_id=1, source_target_pairs={{0,4},{4,8},{8,12},{12,0},{1,5},{5,9},{9,13},{13,1},{2,6},{6,10},{... | collective-permute-start | bytes 36872 | tf_op jit(solution)/shard_map/ppermute | solution.py:14
  48.9 12.0 %collective-permute-start.7 = (f32[3,4,256]{2,0,1:T(4,128)S(1)}, f32[3,4,256]{2,0,1:T(4,128)S(1)}, u32[]{:S(2)}, u32[]{:S(2)}) collective-permute-start(f32[3,4,256]{2,0,1:T(4,128)S(1)} %constant_dynamic-update-slice_fusion.8), channel_id=1, source_target_pairs={{0,8},{4,12},{8,0},{12,4},{1,9},{5,13},{9,1},{13,5},{2,10},{6,14},... | collective-permute-start | bytes 36872 | tf_op jit(solution)/shard_map/ppermute | solution.py:14
  50.3 10.6 %collective-permute-start.8 = (f32[3,4,256]{2,0,1:T(4,128)S(1)}, f32[3,4,256]{2,0,1:T(4,128)S(1)}, u32[]{:S(2)}, u32[]{:S(2)}) collective-permute-start(f32[3,4,256]{2,0,1:T(4,128)S(1)} %constant_dynamic-update-slice_fusion.8), channel_id=1, source_target_pairs={{0,12},{4,0},{8,4},{12,8},{1,13},{5,1},{9,5},{13,9},{2,14},{6,2},{... | collective-permute-start | bytes 36872 | tf_op jit(solution)/shard_map/ppermute | solution.py:14
  55.7 10.0 %collective-permute-start.21 = (f32[3,4,256]{2,0,1:T(4,128)S(1)}, f32[3,4,256]{2,0,1:T(4,128)S(1)}, u32[]{:S(2)}, u32[]{:S(2)}) collective-permute-start(f32[3,4,256]{2,0,1:T(4,128)S(1)} %constant_dynamic-update-slice_fusion.28), channel_id=1, source_target_pairs={{0,4},{4,8},{8,12},{12,0},{1,5},{5,9},{9,13},{13,1},{2,6},{6,10},{... | collective-permute-start | bytes 36872 | tf_op jit(solution)/shard_map/ppermute | solution.py:14
  56.3 10.6 %collective-permute-start.22 = (f32[3,4,256]{2,0,1:T(4,128)S(1)}, f32[3,4,256]{2,0,1:T(4,128)S(1)}, u32[]{:S(2)}, u32[]{:S(2)}) collective-permute-start(f32[3,4,256]{2,0,1:T(4,128)S(1)} %constant_dynamic-update-slice_fusion.28), channel_id=1, source_target_pairs={{0,8},{4,12},{8,0},{12,4},{1,9},{5,13},{9,1},{13,5},{2,10},{6,14},... | collective-permute-start | bytes 36872 | tf_op jit(solution)/shard_map/ppermute | solution.py:14
  58.0 8.9 %collective-permute-start.23 = (f32[3,4,256]{2,0,1:T(4,128)S(1)}, f32[3,4,256]{2,0,1:T(4,128)S(1)}, u32[]{:S(2)}, u32[]{:S(2)}) collective-permute-start(f32[3,4,256]{2,0,1:T(4,128)S(1)} %constant_dynamic-update-slice_fusion.28), channel_id=1, source_target_pairs={{0,12},{4,0},{8,4},{12,8},{1,13},{5,1},{9,5},{13,9},{2,14},{6,2},{... | collective-permute-start | bytes 36872 | tf_op jit(solution)/shard_map/ppermute | solution.py:14
  63.3 24.3 %collective-permute-start.10 = (f32[3,4,256]{2,0,1:T(4,128)S(1)}, f32[3,4,256]{2,0,1:T(4,128)S(1)}, u32[]{:S(2)}, u32[]{:S(2)}) collective-permute-start(f32[3,4,256]{2,0,1:T(4,128)S(1)} %constant_dynamic-update-slice_fusion.12), channel_id=1, source_target_pairs={{0,8},{4,12},{8,0},{12,4},{1,9},{5,13},{9,1},{13,5},{2,10},{6,14},... | collective-permute-start | bytes 36872 | tf_op jit(solution)/shard_map/ppermute | solution.py:14
  64.3 23.3 %collective-permute-start.11 = (f32[3,4,256]{2,0,1:T(4,128)S(1)}, f32[3,4,256]{2,0,1:T(4,128)S(1)}, u32[]{:S(2)}, u32[]{:S(2)}) collective-permute-start(f32[3,4,256]{2,0,1:T(4,128)S(1)} %constant_dynamic-update-slice_fusion.12), channel_id=1, source_target_pairs={{0,12},{4,0},{8,4},{12,8},{1,13},{5,1},{9,5},{13,9},{2,14},{6,2},{... | collective-permute-start | bytes 36872 | tf_op jit(solution)/shard_map/ppermute | solution.py:14
  65.7 21.9 %collective-permute-start.9 = (f32[3,4,256]{2,0,1:T(4,128)S(1)}, f32[3,4,256]{2,0,1:T(4,128)S(1)}, u32[]{:S(2)}, u32[]{:S(2)}) collective-permute-start(f32[3,4,256]{2,0,1:T(4,128)S(1)} %constant_dynamic-update-slice_fusion.12), channel_id=1, source_target_pairs={{0,4},{4,8},{8,12},{12,0},{1,5},{5,9},{9,13},{13,1},{2,6},{6,10},{... | collective-permute-start | bytes 36872 | tf_op jit(solution)/shard_map/ppermute | solution.py:14
  (4 other events, 23.0 us)
where the time goes:
time: 90.1 us; the launch traced here: 89.9 us
  starting transfers between devices  36.9 us (41%)
  blocking collectives  23.9 us (27%)
  local copies, waits for them, and re-layouts  22.3 us (25%)
  matrix products  2.63 us (3%)
  other arithmetic  2.6 us (3%)
  between operations  1.55 us (2%)
    ppermute x24, starting transfers between devices, from_behind(): return lax.ppermute(value, axis, pairs)  36.9 us
    psum x1, blocking collectives, tile_total(): return lax.psum(filter_part, 'tile')  18.3 us
    all_gather x1, blocking collectives, on_device(): whole_grad = lax.all_gather(out_grad, 'sub', axis=1, tiled=True)  5.58 us
    gather x8, local copies, waits for them, and re-layouts, laplace(): ghosts = stacked[local_rows, my_edges]  4.87 us
    another operation x40, local copies, waits for them, and re-layouts, edge_lines(): jnp.stack([values[..., :tile_side], values[..., -tile_side:], values[...,...  2.57 us
  transfers between devices with their start and end apart: 24, of which 0 were waited for; matrix products, arithmetic and copies ran while one was open for 26% of the time, Pallas kernels for 0%

commit v1 on v0

--- a/solution.py
+++ b/solution.py
@@ -151,7 +151,7 @@
 
 
 def tile_total(filter_part):
-    return lax.psum(filter_part, "tile")
+    return jnp.sum(lax.all_gather(filter_part, "tile"), axis=0)
 
 
 def on_device(features, out_grad, filters, tile_map):

time: 90.1 us -> 85 us (0.943)
  blocking collectives: 23.9 us -> 18.8 us
    psum x1 -> x0, blocking collectives: 18.3 us -> none  [tile_total(): return lax.psum(filter_part, 'tile')]
    all_gather x0 -> x1, blocking collectives: none -> 13.2 us  [tile_total(): return jnp.sum(lax.all_gather(filter_part, 'tile'), axis=0)]
  transfers between devices with their start and end apart: 24 -> 24, of which waited for: 0 -> 0; matrix products, arithmetic and copies ran while one was open for 26% -> 27% of each run, Pallas kernels for 0% -> 0%
where the time goes in v1:
time: 85 us; the launch traced here: 84.8 us
  starting transfers between devices  36.9 us (43%)
  local copies, waits for them, and re-layouts  22.3 us (26%)
  blocking collectives  18.8 us (22%)
  matrix products  2.63 us (3%)
  other arithmetic  2.61 us (3%)
  between operations  1.55 us (2%)
    ppermute x24, starting transfers between devices, from_behind(): return lax.ppermute(value, axis, pairs)  36.9 us
    all_gather x1, blocking collectives, tile_total(): return jnp.sum(lax.all_gather(filter_part, 'tile'), axis=0)  13.2 us
    all_gather x1, blocking collectives, on_device(): whole_grad = lax.all_gather(out_grad, 'sub', axis=1, tiled=True)  5.58 us
    gather x8, local copies, waits for them, and re-layouts, laplace(): ghosts = stacked[local_rows, my_edges]  4.87 us
    another operation x40, local copies, waits for them, and re-layouts, edge_lines(): jnp.stack([values[..., :tile_side], values[..., -tile_side:], values[...,...  2.57 us
  transfers between devices with their start and end apart: 24, of which 0 were waited for; matrix products, arithmetic and copies ran while one was open for 27% of the time, Pallas kernels for 0%

profile of v1, /device:TPU:0, one launch (start us, length us, event | category | flops | bytes accessed | tf_op | source)
XLA Modules:
  0.0 84.8 jit_solution(2871885318123559040)
XLA Ops:
  0.7 0.8 fusion.100
  2.1 3.1 %collective-permute-start.12 = (f32[3,4,256]{2,0,1:T(4,128)S(1)}, f32[3,4,256]{2,0,1:T(4,128)S(1)}, u32[]{:S(2)}, u32[]{:S(2)}) collective-permute-start(f32[3,4,256]{2,0,1:T(4,128)S(1)} %constant_dynamic-update-slice_fusion.16), channel_id=1, source_target_pairs={{0,4},{4,8},{8,12},{12,0},{1,5},{5,9},{9,13},{13,1},{2,6},{6,10},{... | collective-permute-start | bytes 36872 | tf_op jit(solution)/shard_map/ppermute | solution.py:14
  5.2 2.6 %collective-permute-start.13 = (f32[3,4,256]{2,0,1:T(4,128)S(1)}, f32[3,4,256]{2,0,1:T(4,128)S(1)}, u32[]{:S(2)}, u32[]{:S(2)}) collective-permute-start(f32[3,4,256]{2,0,1:T(4,128)S(1)} %constant_dynamic-update-slice_fusion.16), channel_id=1, source_target_pairs={{0,8},{4,12},{8,0},{12,4},{1,9},{5,13},{9,1},{13,5},{2,10},{6,14},... | collective-permute-start | bytes 36872 | tf_op jit(solution)/shard_map/ppermute | solution.py:14
  7.8 1.3 %collective-permute-start.14 = (f32[3,4,256]{2,0,1:T(4,128)S(1)}, f32[3,4,256]{2,0,1:T(4,128)S(1)}, u32[]{:S(2)}, u32[]{:S(2)}) collective-permute-start(f32[3,4,256]{2,0,1:T(4,128)S(1)} %constant_dynamic-update-slice_fusion.16), channel_id=1, source_target_pairs={{0,12},{4,0},{8,4},{12,8},{1,13},{5,1},{9,5},{13,9},{2,14},{6,2},{... | collective-permute-start | bytes 36872 | tf_op jit(solution)/shard_map/ppermute | solution.py:14
  9.2 5.6 %all_gather.9 = bf16[3,32,1024]{2,1,0:T(8,128)(2,1)S(1)} all-gather(bf16[3,8,1024]{2,1,0:T(8,128)(2,1)S(1)} %copy-done.2), channel_id=1, replica_groups=mesh['grp'=2,'tile'=4,'sub'=4] {'sub'}, dimensions={1}, use_global_device_ids=true | all-gather | bytes 245760 | tf_op jit(solution)/shard_map/all_gather | solution.py:187
  15.7 0.7 collective-permute-start
  18.3 1.2 %sort.17 = (s32[12]{0:T(128)}, s32[12]{0:T(128)S(1)}) sort(s32[12]{0:T(128)S(1)} %copy-done.3, s32[12]{0:T(128)S(1)} %iota.45), dimensions={0}, to_apply=%region_0.1 | sort | flops 48 | bytes 192 | tf_op jit(solution)/shard_map/jit(argsort)/sort | solution.py:107
  19.5 0.8 gather_fusion
  21.4 2.8 %collective-permute-start.2 = (f32[3,4,256]{2,0,1:T(4,128)S(1)}, f32[3,4,256]{2,0,1:T(4,128)S(1)}, u32[]{:S(2)}, u32[]{:S(2)}) collective-permute-start(f32[3,4,256]{2,0,1:T(4,128)S(1)} %constant_dynamic-update-slice_fusion), channel_id=1, source_target_pairs={{0,12},{4,0},{8,4},{12,8},{1,13},{5,1},{9,5},{13,9},{2,14},{6,2},{... | collective-permute-start | bytes 36872 | tf_op jit(solution)/shard_map/ppermute | solution.py:14
  27.3 1.5 %collective-permute-start.16 = (f32[3,4,256]{2,0,1:T(4,128)S(1)}, f32[3,4,256]{2,0,1:T(4,128)S(1)}, u32[]{:S(2)}, u32[]{:S(2)}) collective-permute-start(f32[3,4,256]{2,0,1:T(4,128)S(1)} %constant_dynamic-update-slice_fusion.20), channel_id=1, source_target_pairs={{0,8},{4,12},{8,0},{12,4},{1,9},{5,13},{9,1},{13,5},{2,10},{6,14},... | collective-permute-start | bytes 36872 | tf_op jit(solution)/shard_map/ppermute | solution.py:14
  29.0 2.9 %collective-permute-start.17 = (f32[3,4,256]{2,0,1:T(4,128)S(1)}, f32[3,4,256]{2,0,1:T(4,128)S(1)}, u32[]{:S(2)}, u32[]{:S(2)}) collective-permute-start(f32[3,4,256]{2,0,1:T(4,128)S(1)} %constant_dynamic-update-slice_fusion.20), channel_id=1, source_target_pairs={{0,12},{4,0},{8,4},{12,8},{1,13},{5,1},{9,5},{13,9},{2,14},{6,2},{... | collective-permute-start | bytes 36872 | tf_op jit(solution)/shard_map/ppermute | solution.py:14
  34.4 1.0 %collective-permute-start.4 = (f32[3,4,256]{2,0,1:T(4,128)S(1)}, f32[3,4,256]{2,0,1:T(4,128)S(1)}, u32[]{:S(2)}, u32[]{:S(2)}) collective-permute-start(f32[3,4,256]{2,0,1:T(4,128)S(1)} %constant_dynamic-update-slice_fusion.4), channel_id=1, source_target_pairs={{0,8},{4,12},{8,0},{12,4},{1,9},{5,13},{9,1},{13,5},{2,10},{6,14},... | collective-permute-start | bytes 36872 | tf_op jit(solution)/shard_map/ppermute | solution.py:14
  35.8 2.9 %collective-permute-start.5 = (f32[3,4,256]{2,0,1:T(4,128)S(1)}, f32[3,4,256]{2,0,1:T(4,128)S(1)}, u32[]{:S(2)}, u32[]{:S(2)}) collective-permute-start(f32[3,4,256]{2,0,1:T(4,128)S(1)} %constant_dynamic-update-slice_fusion.4), channel_id=1, source_target_pairs={{0,12},{4,0},{8,4},{12,8},{1,13},{5,1},{9,5},{13,9},{2,14},{6,2},{... | collective-permute-start | bytes 36872 | tf_op jit(solution)/shard_map/ppermute | solution.py:14
  41.8 1.5 %collective-permute-start.19 = (f32[3,4,256]{2,0,1:T(4,128)S(1)}, f32[3,4,256]{2,0,1:T(4,128)S(1)}, u32[]{:S(2)}, u32[]{:S(2)}) collective-permute-start(f32[3,4,256]{2,0,1:T(4,128)S(1)} %constant_dynamic-update-slice_fusion.24), channel_id=1, source_target_pairs={{0,8},{4,12},{8,0},{12,4},{1,9},{5,13},{9,1},{13,5},{2,10},{6,14},... | collective-permute-start | bytes 36872 | tf_op jit(solution)/shard_map/ppermute | solution.py:14
  43.5 2.9 %collective-permute-start.20 = (f32[3,4,256]{2,0,1:T(4,128)S(1)}, f32[3,4,256]{2,0,1:T(4,128)S(1)}, u32[]{:S(2)}, u32[]{:S(2)}) collective-permute-start(f32[3,4,256]{2,0,1:T(4,128)S(1)} %constant_dynamic-update-slice_fusion.24), channel_id=1, source_target_pairs={{0,12},{4,0},{8,4},{12,8},{1,13},{5,1},{9,5},{13,9},{2,14},{6,2},{... | collective-permute-start | bytes 36872 | tf_op jit(solution)/shard_map/ppermute | solution.py:14
  48.9 1.0 %collective-permute-start.7 = (f32[3,4,256]{2,0,1:T(4,128)S(1)}, f32[3,4,256]{2,0,1:T(4,128)S(1)}, u32[]{:S(2)}, u32[]{:S(2)}) collective-permute-start(f32[3,4,256]{2,0,1:T(4,128)S(1)} %constant_dynamic-update-slice_fusion.8), channel_id=1, source_target_pairs={{0,8},{4,12},{8,0},{12,4},{1,9},{5,13},{9,1},{13,5},{2,10},{6,14},... | collective-permute-start | bytes 36872 | tf_op jit(solution)/shard_map/ppermute | solution.py:14
  50.3 2.9 %collective-permute-start.8 = (f32[3,4,256]{2,0,1:T(4,128)S(1)}, f32[3,4,256]{2,0,1:T(4,128)S(1)}, u32[]{:S(2)}, u32[]{:S(2)}) collective-permute-start(f32[3,4,256]{2,0,1:T(4,128)S(1)} %constant_dynamic-update-slice_fusion.8), channel_id=1, source_target_pairs={{0,12},{4,0},{8,4},{12,8},{1,13},{5,1},{9,5},{13,9},{2,14},{6,2},{... | collective-permute-start | bytes 36872 | tf_op jit(solution)/shard_map/ppermute | solution.py:14
  56.3 1.5 %collective-permute-start.22 = (f32[3,4,256]{2,0,1:T(4,128)S(1)}, f32[3,4,256]{2,0,1:T(4,128)S(1)}, u32[]{:S(2)}, u32[]{:S(2)}) collective-permute-start(f32[3,4,256]{2,0,1:T(4,128)S(1)} %constant_dynamic-update-slice_fusion.28), channel_id=1, source_target_pairs={{0,8},{4,12},{8,0},{12,4},{1,9},{5,13},{9,1},{13,5},{2,10},{6,14},... | collective-permute-start | bytes 36872 | tf_op jit(solution)/shard_map/ppermute | solution.py:14
  58.0 2.9 %collective-permute-start.23 = (f32[3,4,256]{2,0,1:T(4,128)S(1)}, f32[3,4,256]{2,0,1:T(4,128)S(1)}, u32[]{:S(2)}, u32[]{:S(2)}) collective-permute-start(f32[3,4,256]{2,0,1:T(4,128)S(1)} %constant_dynamic-update-slice_fusion.28), channel_id=1, source_target_pairs={{0,12},{4,0},{8,4},{12,8},{1,13},{5,1},{9,5},{13,9},{2,14},{6,2},{... | collective-permute-start | bytes 36872 | tf_op jit(solution)/shard_map/ppermute | solution.py:14
  63.3 1.0 %collective-permute-start.10 = (f32[3,4,256]{2,0,1:T(4,128)S(1)}, f32[3,4,256]{2,0,1:T(4,128)S(1)}, u32[]{:S(2)}, u32[]{:S(2)}) collective-permute-start(f32[3,4,256]{2,0,1:T(4,128)S(1)} %constant_dynamic-update-slice_fusion.12), channel_id=1, source_target_pairs={{0,8},{4,12},{8,0},{12,4},{1,9},{5,13},{9,1},{13,5},{2,10},{6,14},... | collective-permute-start | bytes 36872 | tf_op jit(solution)/shard_map/ppermute | solution.py:14
  64.3 0.9 %collective-permute-start.11 = (f32[3,4,256]{2,0,1:T(4,128)S(1)}, f32[3,4,256]{2,0,1:T(4,128)S(1)}, u32[]{:S(2)}, u32[]{:S(2)}) collective-permute-start(f32[3,4,256]{2,0,1:T(4,128)S(1)} %constant_dynamic-update-slice_fusion.12), channel_id=1, source_target_pairs={{0,12},{4,0},{8,4},{12,8},{1,13},{5,1},{9,5},{13,9},{2,14},{6,2},{... | collective-permute-start | bytes 36872 | tf_op jit(solution)/shard_map/ppermute | solution.py:14
  65.7 1.1 %collective-permute-start.9 = (f32[3,4,256]{2,0,1:T(4,128)S(1)}, f32[3,4,256]{2,0,1:T(4,128)S(1)}, u32[]{:S(2)}, u32[]{:S(2)}) collective-permute-start(f32[3,4,256]{2,0,1:T(4,128)S(1)} %constant_dynamic-update-slice_fusion.12), channel_id=1, source_target_pairs={{0,4},{4,8},{8,12},{12,0},{1,5},{5,9},{9,13},{13,1},{2,6},{6,10},{... | collective-permute-start | bytes 36872 | tf_op jit(solution)/shard_map/ppermute | solution.py:14
  68.7 13.2 %all-gather = f32[20,8,32]{2,1,0:T(8,128)S(1)} all-gather(f32[5,8,32]{2,1,0:T(8,128)S(1)} %fusion.8), channel_id=2, replica_groups=mesh['grp'=2,'tile'=4,'sub'=4] {'tile'}, dimensions={0}, use_global_device_ids=true | all-gather | bytes 25600 | tf_op jit(solution)/shard_map/all_gather | solution.py:154
  84.0 0.8 fusion.7
  (248 shorter events, 26.3 us)
Async XLA Ops:
  2.1 19.3 %collective-permute-start.12 = (f32[3,4,256]{2,0,1:T(4,128)S(1)}, f32[3,4,256]{2,0,1:T(4,128)S(1)}, u32[]{:S(2)}, u32[]{:S(2)}) collective-permute-start(f32[3,4,256]{2,0,1:T(4,128)S(1)} %constant_dynamic-update-slice_fusion.16), channel_id=1, source_target_pairs={{0,4},{4,8},{8,12},{12,0},{1,5},{5,9},{9,13},{13,1},{2,6},{6,10},{... | collective-permute-start | bytes 36872 | tf_op jit(solution)/shard_map/ppermute | solution.py:14
  5.2 19.0 %collective-permute-start.13 = (f32[3,4,256]{2,0,1:T(4,128)S(1)}, f32[3,4,256]{2,0,1:T(4,128)S(1)}, u32[]{:S(2)}, u32[]{:S(2)}) collective-permute-start(f32[3,4,256]{2,0,1:T(4,128)S(1)} %constant_dynamic-update-slice_fusion.16), channel_id=1, source_target_pairs={{0,8},{4,12},{8,0},{12,4},{1,9},{5,13},{9,1},{13,5},{2,10},{6,14},... | collective-permute-start | bytes 36872 | tf_op jit(solution)/shard_map/ppermute | solution.py:14
  7.8 16.4 %collective-permute-start.14 = (f32[3,4,256]{2,0,1:T(4,128)S(1)}, f32[3,4,256]{2,0,1:T(4,128)S(1)}, u32[]{:S(2)}, u32[]{:S(2)}) collective-permute-start(f32[3,4,256]{2,0,1:T(4,128)S(1)} %constant_dynamic-update-slice_fusion.16), channel_id=1, source_target_pairs={{0,12},{4,0},{8,4},{12,8},{1,13},{5,1},{9,5},{13,9},{2,14},{6,2},{... | collective-permute-start | bytes 36872 | tf_op jit(solution)/shard_map/ppermute | solution.py:14
  15.7 13.3 %collective-permute-start = (f32[3,4,256]{2,0,1:T(4,128)S(1)}, f32[3,4,256]{2,0,1:T(4,128)S(1)}, u32[]{:S(2)}, u32[]{:S(2)}) collective-permute-start(f32[3,4,256]{2,0,1:T(4,128)S(1)} %constant_dynamic-update-slice_fusion), channel_id=1, source_target_pairs={{0,4},{4,8},{8,12},{12,0},{1,5},{5,9},{9,13},{13,1},{2,6},{6,10},{... | collective-permute-start | bytes 36872 | tf_op jit(solution)/shard_map/ppermute | solution.py:14
  16.4 15.5 %collective-permute-start.1 = (f32[3,4,256]{2,0,1:T(4,128)S(1)}, f32[3,4,256]{2,0,1:T(4,128)S(1)}, u32[]{:S(2)}, u32[]{:S(2)}) collective-permute-start(f32[3,4,256]{2,0,1:T(4,128)S(1)} %constant_dynamic-update-slice_fusion), channel_id=1, source_target_pairs={{0,8},{4,12},{8,0},{12,4},{1,9},{5,13},{9,1},{13,5},{2,10},{6,14},... | collective-permute-start | bytes 36872 | tf_op jit(solution)/shard_map/ppermute | solution.py:14
  21.4 10.5 %collective-permute-start.2 = (f32[3,4,256]{2,0,1:T(4,128)S(1)}, f32[3,4,256]{2,0,1:T(4,128)S(1)}, u32[]{:S(2)}, u32[]{:S(2)}) collective-permute-start(f32[3,4,256]{2,0,1:T(4,128)S(1)} %constant_dynamic-update-slice_fusion), channel_id=1, source_target_pairs={{0,12},{4,0},{8,4},{12,8},{1,13},{5,1},{9,5},{13,9},{2,14},{6,2},{... | collective-permute-start | bytes 36872 | tf_op jit(solution)/shard_map/ppermute | solution.py:14
  26.7 9.2 %collective-permute-start.15 = (f32[3,4,256]{2,0,1:T(4,128)S(1)}, f32[3,4,256]{2,0,1:T(4,128)S(1)}, u32[]{:S(2)}, u32[]{:S(2)}) collective-permute-start(f32[3,4,256]{2,0,1:T(4,128)S(1)} %constant_dynamic-update-slice_fusion.20), channel_id=1, source_target_pairs={{0,4},{4,8},{8,12},{12,0},{1,5},{5,9},{9,13},{13,1},{2,6},{6,10},{... | collective-permute-start | bytes 36872 | tf_op jit(solution)/shard_map/ppermute | solution.py:14
  27.3 11.4 %collective-permute-start.16 = (f32[3,4,256]{2,0,1:T(4,128)S(1)}, f32[3,4,256]{2,0,1:T(4,128)S(1)}, u32[]{:S(2)}, u32[]{:S(2)}) collective-permute-start(f32[3,4,256]{2,0,1:T(4,128)S(1)} %constant_dynamic-update-slice_fusion.20), channel_id=1, source_target_pairs={{0,8},{4,12},{8,0},{12,4},{1,9},{5,13},{9,1},{13,5},{2,10},{6,14},... | collective-permute-start | bytes 36872 | tf_op jit(solution)/shard_map/ppermute | solution.py:14
  29.0 9.7 %collective-permute-start.17 = (f32[3,4,256]{2,0,1:T(4,128)S(1)}, f32[3,4,256]{2,0,1:T(4,128)S(1)}, u32[]{:S(2)}, u32[]{:S(2)}) collective-permute-start(f32[3,4,256]{2,0,1:T(4,128)S(1)} %constant_dynamic-update-slice_fusion.20), channel_id=1, source_target_pairs={{0,12},{4,0},{8,4},{12,8},{1,13},{5,1},{9,5},{13,9},{2,14},{6,2},{... | collective-permute-start | bytes 36872 | tf_op jit(solution)/shard_map/ppermute | solution.py:14
  34.3 9.1 %collective-permute-start.3 = (f32[3,4,256]{2,0,1:T(4,128)S(1)}, f32[3,4,256]{2,0,1:T(4,128)S(1)}, u32[]{:S(2)}, u32[]{:S(2)}) collective-permute-start(f32[3,4,256]{2,0,1:T(4,128)S(1)} %constant_dynamic-update-slice_fusion.4), channel_id=1, source_target_pairs={{0,4},{4,8},{8,12},{12,0},{1,5},{5,9},{9,13},{13,1},{2,6},{6,10},{... | collective-permute-start | bytes 36872 | tf_op jit(solution)/shard_map/ppermute | solution.py:14
  34.4 12.0 %collective-permute-start.4 = (f32[3,4,256]{2,0,1:T(4,128)S(1)}, f32[3,4,256]{2,0,1:T(4,128)S(1)}, u32[]{:S(2)}, u32[]{:S(2)}) collective-permute-start(f32[3,4,256]{2,0,1:T(4,128)S(1)} %constant_dynamic-update-slice_fusion.4), channel_id=1, source_target_pairs={{0,8},{4,12},{8,0},{12,4},{1,9},{5,13},{9,1},{13,5},{2,10},{6,14},... | collective-permute-start | bytes 36872 | tf_op jit(solution)/shard_map/ppermute | solution.py:14
  35.8 10.6 %collective-permute-start.5 = (f32[3,4,256]{2,0,1:T(4,128)S(1)}, f32[3,4,256]{2,0,1:T(4,128)S(1)}, u32[]{:S(2)}, u32[]{:S(2)}) collective-permute-start(f32[3,4,256]{2,0,1:T(4,128)S(1)} %constant_dynamic-update-slice_fusion.4), channel_id=1, source_target_pairs={{0,12},{4,0},{8,4},{12,8},{1,13},{5,1},{9,5},{13,9},{2,14},{6,2},{... | collective-permute-start | bytes 36872 | tf_op jit(solution)/shard_map/ppermute | solution.py:14
  41.2 9.2 %collective-permute-start.18 = (f32[3,4,256]{2,0,1:T(4,128)S(1)}, f32[3,4,256]{2,0,1:T(4,128)S(1)}, u32[]{:S(2)}, u32[]{:S(2)}) collective-permute-start(f32[3,4,256]{2,0,1:T(4,128)S(1)} %constant_dynamic-update-slice_fusion.24), channel_id=1, source_target_pairs={{0,4},{4,8},{8,12},{12,0},{1,5},{5,9},{9,13},{13,1},{2,6},{6,10},{... | collective-permute-start | bytes 36872 | tf_op jit(solution)/shard_map/ppermute | solution.py:14
  41.8 11.4 %collective-permute-start.19 = (f32[3,4,256]{2,0,1:T(4,128)S(1)}, f32[3,4,256]{2,0,1:T(4,128)S(1)}, u32[]{:S(2)}, u32[]{:S(2)}) collective-permute-start(f32[3,4,256]{2,0,1:T(4,128)S(1)} %constant_dynamic-update-slice_fusion.24), channel_id=1, source_target_pairs={{0,8},{4,12},{8,0},{12,4},{1,9},{5,13},{9,1},{13,5},{2,10},{6,14},... | collective-permute-start | bytes 36872 | tf_op jit(solution)/shard_map/ppermute | solution.py:14
  43.5 9.7 %collective-permute-start.20 = (f32[3,4,256]{2,0,1:T(4,128)S(1)}, f32[3,4,256]{2,0,1:T(4,128)S(1)}, u32[]{:S(2)}, u32[]{:S(2)}) collective-permute-start(f32[3,4,256]{2,0,1:T(4,128)S(1)} %constant_dynamic-update-slice_fusion.24), channel_id=1, source_target_pairs={{0,12},{4,0},{8,4},{12,8},{1,13},{5,1},{9,5},{13,9},{2,14},{6,2},{... | collective-permute-start | bytes 36872 | tf_op jit(solution)/shard_map/ppermute | solution.py:14
  48.8 9.1 %collective-permute-start.6 = (f32[3,4,256]{2,0,1:T(4,128)S(1)}, f32[3,4,256]{2,0,1:T(4,128)S(1)}, u32[]{:S(2)}, u32[]{:S(2)}) collective-permute-start(f32[3,4,256]{2,0,1:T(4,128)S(1)} %constant_dynamic-update-slice_fusion.8), channel_id=1, source_target_pairs={{0,4},{4,8},{8,12},{12,0},{1,5},{5,9},{9,13},{13,1},{2,6},{6,10},{... | collective-permute-start | bytes 36872 | tf_op jit(solution)/shard_map/ppermute | solution.py:14
  48.9 12.0 %collective-permute-start.7 = (f32[3,4,256]{2,0,1:T(4,128)S(1)}, f32[3,4,256]{2,0,1:T(4,128)S(1)}, u32[]{:S(2)}, u32[]{:S(2)}) collective-permute-start(f32[3,4,256]{2,0,1:T(4,128)S(1)} %constant_dynamic-update-slice_fusion.8), channel_id=1, source_target_pairs={{0,8},{4,12},{8,0},{12,4},{1,9},{5,13},{9,1},{13,5},{2,10},{6,14},... | collective-permute-start | bytes 36872 | tf_op jit(solution)/shard_map/ppermute | solution.py:14
  50.3 10.6 %collective-permute-start.8 = (f32[3,4,256]{2,0,1:T(4,128)S(1)}, f32[3,4,256]{2,0,1:T(4,128)S(1)}, u32[]{:S(2)}, u32[]{:S(2)}) collective-permute-start(f32[3,4,256]{2,0,1:T(4,128)S(1)} %constant_dynamic-update-slice_fusion.8), channel_id=1, source_target_pairs={{0,12},{4,0},{8,4},{12,8},{1,13},{5,1},{9,5},{13,9},{2,14},{6,2},{... | collective-permute-start | bytes 36872 | tf_op jit(solution)/shard_map/ppermute | solution.py:14
  55.7 10.0 %collective-permute-start.21 = (f32[3,4,256]{2,0,1:T(4,128)S(1)}, f32[3,4,256]{2,0,1:T(4,128)S(1)}, u32[]{:S(2)}, u32[]{:S(2)}) collective-permute-start(f32[3,4,256]{2,0,1:T(4,128)S(1)} %constant_dynamic-update-slice_fusion.28), channel_id=1, source_target_pairs={{0,4},{4,8},{8,12},{12,0},{1,5},{5,9},{9,13},{13,1},{2,6},{6,10},{... | collective-permute-start | bytes 36872 | tf_op jit(solution)/shard_map/ppermute | solution.py:14
  56.3 10.6 %collective-permute-start.22 = (f32[3,4,256]{2,0,1:T(4,128)S(1)}, f32[3,4,256]{2,0,1:T(4,128)S(1)}, u32[]{:S(2)}, u32[]{:S(2)}) collective-permute-start(f32[3,4,256]{2,0,1:T(4,128)S(1)} %constant_dynamic-update-slice_fusion.28), channel_id=1, source_target_pairs={{0,8},{4,12},{8,0},{12,4},{1,9},{5,13},{9,1},{13,5},{2,10},{6,14},... | collective-permute-start | bytes 36872 | tf_op jit(solution)/shard_map/ppermute | solution.py:14
  58.0 8.9 %collective-permute-start.23 = (f32[3,4,256]{2,0,1:T(4,128)S(1)}, f32[3,4,256]{2,0,1:T(4,128)S(1)}, u32[]{:S(2)}, u32[]{:S(2)}) collective-permute-start(f32[3,4,256]{2,0,1:T(4,128)S(1)} %constant_dynamic-update-slice_fusion.28), channel_id=1, source_target_pairs={{0,12},{4,0},{8,4},{12,8},{1,13},{5,1},{9,5},{13,9},{2,14},{6,2},{... | collective-permute-start | bytes 36872 | tf_op jit(solution)/shard_map/ppermute | solution.py:14
  63.3 19.2 %collective-permute-start.10 = (f32[3,4,256]{2,0,1:T(4,128)S(1)}, f32[3,4,256]{2,0,1:T(4,128)S(1)}, u32[]{:S(2)}, u32[]{:S(2)}) collective-permute-start(f32[3,4,256]{2,0,1:T(4,128)S(1)} %constant_dynamic-update-slice_fusion.12), channel_id=1, source_target_pairs={{0,8},{4,12},{8,0},{12,4},{1,9},{5,13},{9,1},{13,5},{2,10},{6,14},... | collective-permute-start | bytes 36872 | tf_op jit(solution)/shard_map/ppermute | solution.py:14
  64.3 18.2 %collective-permute-start.11 = (f32[3,4,256]{2,0,1:T(4,128)S(1)}, f32[3,4,256]{2,0,1:T(4,128)S(1)}, u32[]{:S(2)}, u32[]{:S(2)}) collective-permute-start(f32[3,4,256]{2,0,1:T(4,128)S(1)} %constant_dynamic-update-slice_fusion.12), channel_id=1, source_target_pairs={{0,12},{4,0},{8,4},{12,8},{1,13},{5,1},{9,5},{13,9},{2,14},{6,2},{... | collective-permute-start | bytes 36872 | tf_op jit(solution)/shard_map/ppermute | solution.py:14
  65.7 16.8 %collective-permute-start.9 = (f32[3,4,256]{2,0,1:T(4,128)S(1)}, f32[3,4,256]{2,0,1:T(4,128)S(1)}, u32[]{:S(2)}, u32[]{:S(2)}) collective-permute-start(f32[3,4,256]{2,0,1:T(4,128)S(1)} %constant_dynamic-update-slice_fusion.12), channel_id=1, source_target_pairs={{0,4},{4,8},{8,12},{12,0},{1,5},{5,9},{9,13},{13,1},{2,6},{6,10},{... | collective-permute-start | bytes 36872 | tf_op jit(solution)/shard_map/ppermute | solution.py:14
  (4 other events, 23.0 us)
